TPU v7x, 1024 devices: a whole 8x8x8 slice. The times are simulated.
1024 devices in a mesh: wide: 32 (over z, x_hi), mid: 16 (over y, core), low: 2 (over x_lo).
Axes of the slice: x: 8 (x_hi: 4, x_lo: 2; x = x_hi * 2 + x_lo), y: 8, z: 8, core: 2. Of those that a mesh axis runs over, the one named last changes fastest.
Arguments:
- state: float32 [2, 32, 16, 2, 16384], P(None, 'wide', 'mid', 'low'), may hold values from -6 to 6
- gates: float32 [10, 2, 128, 128], replicated, may hold values from -0.375 to 0.375
- phase_low: float32 [128], replicated, may hold values from -3.140625 to 3.140625
- phase_mid: float32 [128], replicated, may hold values from -3.140625 to 3.140625
- phase_top: float32 [32, 16, 2, 1], P('wide', 'mid', 'low'), may hold values from -3.140625 to 3.140625
- swap_qubits: int32 [2], replicated, may hold values from 0 to 2, as said below
- regroup_order: int32 [4], replicated, may hold values from 0 to 3, each once
Outputs:
- final_state: float32 [2, 32, 16, 2, 16384], P(None, 'wide', 'mid', 'low')
Inputs may be any that keep to these rules, and one draw needn't show every extreme that they name: `swap_qubits`: the two entries differ, and one of them is 2. `regroup_order`: each of 0 to 3 once.
All inputs are finite; a program needn't handle non-finite values.
Results may differ from a plain program's by a relative error of at most 0.0003.
Values sent between devices are 32-bit elements; how exact they have to be, the bound alone decides.
A program may use at most 32 MiB of HBM per device.

v0:
```python
import jax
import jax.numpy as jnp
from jax import lax
from jax.sharding import PartitionSpec as P

HIGH = lax.Precision.HIGHEST


def partner(value, axis, stride):
    mask = 2**stride
    pairs = [(source, source ^ mask) for source in range(lax.axis_size(axis))]
    return lax.ppermute(value, axis, pairs)


def gate_inner(vector, real_gate, imag_gate):

    def product(values, matrix):
        return jnp.einsum("...b,ab->...a", values, matrix, precision=HIGH)

    real_part, imag_part = (vector[0], vector[1])
    return jnp.stack(
        [
            product(real_part, real_gate) - product(imag_part, imag_gate),
            product(real_part, imag_gate) + product(imag_part, real_gate),
        ]
    )


def gate_outer(vector, real_gate, imag_gate):

    def product(values, matrix):
        return jnp.einsum("ab,rbc->rac", matrix, values, precision=HIGH)

    real_part, imag_part = (vector[0], vector[1])
    return jnp.stack(
        [
            product(real_part, real_gate) - product(imag_part, imag_gate),
            product(real_part, imag_gate) + product(imag_part, real_gate),
        ]
    )


def apply_gate(vector, gates, number, gate_len):
    if number % 2 == 0:
        result = gate_inner(vector.reshape(2, -1, gate_len), gates[number, 0], gates[number, 1])
    else:
        result = gate_outer(
            vector.reshape(2, -1, gate_len, gate_len), gates[number, 0], gates[number, 1]
        )
    return result.reshape(2, -1)


def half_rows(vector, offset, base, own_bit, local_len):
    counter = jnp.arange(4, dtype=jnp.int32)
    lower = counter & jnp.left_shift(1, offset) - 1
    higher = jnp.right_shift(counter, offset)
    row_index = jnp.left_shift(higher, offset + 1) | jnp.left_shift(1 - own_bit, offset) | lower
    blocks = vector.reshape(2, local_len >> base + 3, 8, 1 << base)
    return (blocks, row_index, jnp.take(blocks, row_index, axis=2))


def on_device(state, gates, phase_low, phase_mid, phase_top, swap_qubits, regroup_order):
    local_len = state.shape[-1]
    gate_len = gates.shape[-1]
    gate_count = gates.shape[0]
    local_bits = local_len.bit_length() - 1
    upper_len = local_len // (gate_len * gate_len)
    wide_count = lax.axis_size("wide")
    wide_bits = wide_count.bit_length() - 1
    vector = apply_gate(state.reshape(2, -1), gates, 0, gate_len)
    vector = vector.reshape(2, upper_len, gate_len, gate_len)
    angle = (
        phase_top.reshape(upper_len)[:, None, None]
        + phase_mid[None, :, None]
        + phase_low[None, None, :]
    )
    cosine = jnp.cos(angle)
    sine_part = jnp.sin(angle)
    vector = jnp.stack(
        [vector[0] * cosine - vector[1] * sine_part, vector[0] * sine_part + vector[1] * cosine]
    ).reshape(2, -1)
    for number in range(1, 4):
        vector = apply_gate(vector, gates, number, gate_len)
    mid_bit = lax.axis_index("mid") & 1
    blocks, row_index, sent_half = half_rows(
        vector, swap_qubits[0], local_bits - 3, mid_bit, local_len
    )
    received = partner(sent_half, "mid", 0)
    vector = blocks.at[:, :, row_index].set(received).reshape(2, local_len)
    row_ids = jnp.arange(16, dtype=jnp.int32)[:, None]
    row_bits = jnp.right_shift(row_ids, jnp.arange(4, dtype=jnp.int32)[None, :]) & 1
    order_index = jnp.sum(jnp.left_shift(row_bits, regroup_order[None, :]), axis=1)
    vector = jnp.take(vector.reshape(2, 16, local_len // 16), order_index, axis=1).reshape(
        2, local_len
    )
    low_base = local_bits - wide_bits - 3
    low_bit = lax.axis_index("low") & 1
    blocks, row_index, sent_half = half_rows(vector, swap_qubits[1], low_base, low_bit, local_len)
    received = partner(sent_half, "low", 0)
    vector = blocks.at[:, :, row_index].set(received).reshape(2, local_len)
    for place in range(wide_bits):
        qubit = local_bits - wide_bits + place
        shaped = vector.reshape(2, local_len >> qubit + 1, 2, 1 << qubit)
        own_bit = jnp.right_shift(lax.axis_index("wide"), place) & 1
        sent_half = lax.dynamic_index_in_dim(shaped, 1 - own_bit, 2, keepdims=False)
        received = partner(sent_half, "wide", place)
        shaped = lax.dynamic_update_index_in_dim(shaped, received, 1 - own_bit, 2)
        vector = shaped.reshape(2, local_len)
    for number in range(4, gate_count):
        vector = apply_gate(vector, gates, number, gate_len)
    return vector.reshape(state.shape)


def solution(mesh):
    return jax.shard_map(
        on_device,
        mesh=mesh,
        in_specs=(
            P(None, "wide", "mid", "low", None),
            P(),
            P(),
            P(),
            P("wide", "mid", "low", None),
            P(),
            P(),
        ),
        out_specs=P(None, "wide", "mid", "low", None),
        check_vma=False,
    )
```

profile of v0, /device:TPU:2, one launch (start us, length us, event | category | flops | bytes accessed | tf_op | source)
XLA Modules:
  0.0 97.7 jit_solution(14804759703068167387)
XLA Ops:
  0.0 1.0 %fusion.124 = (f32[1,1,1,1,16384]{4,3,2,1,0:T(1,128)S(1)}, f32[1,1,1,1,16384]{4,3,2,1,0:T(1,128)S(1)}) fusion(f32[2,1,1,1,16384]{4,3,2,1,0:T(1,128)} %param.7), kind=kLoop, calls=%fused_computation.175 | loop fusion | bytes 262144 | tf_op jit(solution)/shard_map/slice | solution.py:20
  1.0 1.1 %fusion.74 = f32[128,128]{1,0:T(8,128)S(1)} fusion(f32[128,128]{1,0:T(8,128)S(1)} %bitcast.242, f32[10,2,128,128]{3,2,1,0:T(8,128)} %param.8), kind=kOutput, calls=%fused_computation.110 | convolution fusion | flops 25165824 | bytes 196608 | tf_op jit(solution)/shard_map/...b,ab->...a/dot_general | solution.py:18
  2.1 1.1 %fusion.70 = f32[128,128]{1,0:T(8,128)S(1)} fusion(f32[128,128]{1,0:T(8,128)S(1)} %bitcast.243, f32[10,2,128,128]{3,2,1,0:T(8,128)} %param.8), kind=kOutput, calls=%fused_computation.106 | convolution fusion | flops 25165824 | bytes 196608 | tf_op jit(solution)/shard_map/...b,ab->...a/dot_general | solution.py:18
  3.2 1.1 %convolution_subtract_fusion.9 = f32[128,128]{1,0:T(8,128)S(1)} fusion(f32[128,128]{1,0:T(8,128)S(1)} %fusion.74, f32[128,128]{1,0:T(8,128)S(1)} %bitcast.244, f32[10,2,128,128]{3,2,1,0:T(8,128)} %param.8), kind=kOutput, calls=%fused_computation.34 | convolution fusion | flops 25182208 | bytes 262144 | tf_op jit(solution)/shard_map/...b,ab->...a/dot_general | solution.py:18
  4.3 1.1 %convolution_add_fusion.9 = f32[128,128]{1,0:T(8,128)S(1)} fusion(f32[128,128]{1,0:T(8,128)S(1)} %fusion.70, f32[128,128]{1,0:T(8,128)S(1)} %bitcast.245, f32[10,2,128,128]{3,2,1,0:T(8,128)} %param.8), kind=kOutput, calls=%fused_computation.33 | convolution fusion | flops 25182208 | bytes 262144 | tf_op jit(solution)/shard_map/...b,ab->...a/dot_general | solution.py:18
  6.1 0.7 broadcast_add_fusion
  6.8 1.4 %fusion.64 = f32[128,128]{1,0:T(8,128)S(1)} fusion(f32[10,2,128,128]{3,2,1,0:T(8,128)} %param.8, f32[128,128]{1,0:T(8,128)S(1)} %convolution_add_fusion.9, f32[128,128]{1,0:T(8,128)S(1)} %convolution_subtract_fusion.9, f32[128]{0:T(128)} %param.9, f32[128]{0:T(128)S(1)} %broadcast_add_fusion), kind=kOutput, calls=%fused_computation.100 | convolution fusion | flops 25231360 | bytes 263168 | tf_op jit(solution)/shard_map/ab,rbc->rac/dot_general | solution.py:32
  8.2 0.6 fusion.68
  8.8 0.6 fusion.9
  9.4 0.3 fusion.58
  9.7 0.3 fusion.62
  10.0 0.6 fusion.8
  10.6 0.3 convolution_subtract_fusion.7
  10.9 0.3 fusion.56
  11.2 0.3 fusion.52
  11.5 0.6 fusion.125
  13.7 0.6 fusion.116
  14.3 0.6 compare_and_fusion.1
  15.2 0.3 fusion.7
  15.6 0.3 fusion.6
  16.1 0.6 gather_fusion
  16.8 1.9 %collective-permute-start = (f32[2,1,4,2048]{3,0,2,1:T(2,128)S(1)}, f32[2,1,4,2048]{3,0,2,1:T(2,128)S(1)}, u32[]{:S(2)}, u32[]{:S(2)}) collective-permute-start(f32[2,1,4,2048]{3,0,2,1:T(2,128)S(1)} %bitcast_select_fusion), channel_id=1, source_target_pairs={{0,2},{2,0},{4,6},{6,4},{8,10},{10,8},{12,14},{14,12},{16,18},{18,... | collective-permute-start | bytes 196616 | tf_op jit(solution)/shard_map/ppermute | solution.py:12
  21.0 0.7 fusion.118
  21.7 0.7 compare_and_fusion
  22.4 0.6 scatter_fusion
  23.0 0.7 gather_fusion.1
  23.9 0.6 gather_fusion.2
  24.6 15.1 %collective-permute-start.1 = (f32[2,32,4,64]{3,1,0,2:T(8,128)S(1)}, f32[2,32,4,64]{3,1,0,2:T(8,128)S(1)}, u32[]{:S(2)}, u32[]{:S(2)}) collective-permute-start(f32[2,32,4,64]{3,1,0,2:T(8,128)S(1)} %select_bitcast_fusion), channel_id=1, source_target_pairs={{0,1},{1,0},{2,3},{3,2},{4,5},{5,4},{6,7},{7,6},{8,9},{9,8},{10,11... | collective-permute-start | bytes 196616 | tf_op jit(solution)/shard_map/ppermute | solution.py:12
  39.7 4.1 %collective-permute-done.1 = f32[2,32,4,64]{3,1,0,2:T(8,128)S(1)} collective-permute-done((f32[2,32,4,64]{3,1,0,2:T(8,128)S(1)}, f32[2,32,4,64]{3,1,0,2:T(8,128)S(1)}, u32[]{:S(2)}, u32[]{:S(2)}) %collective-permute-start.1) | collective-permute-done | bytes 65568 | tf_op jit(solution)/shard_map/ppermute | solution.py:12
  43.8 0.7 scatter_fusion.1
  44.9 1.9 %collective-permute-start.2 = (f32[2,16,512]{2,1,0:T(8,128)S(1)}, f32[2,16,512]{2,1,0:T(8,128)S(1)}, u32[]{:S(2)}, u32[]{:S(2)}) collective-permute-start(f32[2,16,512]{2,1,0:T(8,128)S(1)} %bitcast.255), channel_id=1, source_target_pairs={{0,32},{32,0},{64,96},{96,64},{128,160},{160,128},{192,224},{224,1... | collective-permute-start | bytes 196616 | tf_op jit(solution)/shard_map/ppermute | solution.py:12
  46.8 5.1 %collective-permute-done.2 = f32[2,16,512]{2,1,0:T(8,128)S(1)} collective-permute-done((f32[2,16,512]{2,1,0:T(8,128)S(1)}, f32[2,16,512]{2,1,0:T(8,128)S(1)}, u32[]{:S(2)}, u32[]{:S(2)}) %collective-permute-start.2) | collective-permute-done | bytes 65568 | tf_op jit(solution)/shard_map/ppermute | solution.py:12
  52.0 0.6 dynamic_update_slice.20
  52.9 1.9 %collective-permute-start.3 = (f32[2,8,1024]{2,1,0:T(8,128)S(1)}, f32[2,8,1024]{2,1,0:T(8,128)S(1)}, u32[]{:S(2)}, u32[]{:S(2)}) collective-permute-start(f32[2,8,1024]{2,1,0:T(8,128)S(1)} %bitcast.254), channel_id=1, source_target_pairs={{0,64},{32,96},{64,0},{96,32},{128,192},{160,224},{192,128},{224,1... | collective-permute-start | bytes 196616 | tf_op jit(solution)/shard_map/ppermute | solution.py:12
  54.8 8.1 %collective-permute-done.3 = f32[2,8,1024]{2,1,0:T(8,128)S(1)} collective-permute-done((f32[2,8,1024]{2,1,0:T(8,128)S(1)}, f32[2,8,1024]{2,1,0:T(8,128)S(1)}, u32[]{:S(2)}, u32[]{:S(2)}) %collective-permute-start.3) | collective-permute-done | bytes 65568 | tf_op jit(solution)/shard_map/ppermute | solution.py:12
  63.0 0.5 dynamic_update_slice.21
  63.8 1.9 %collective-permute-start.4 = (f32[2,4,2048]{2,1,0:T(4,128)S(1)}, f32[2,4,2048]{2,1,0:T(4,128)S(1)}, u32[]{:S(2)}, u32[]{:S(2)}) collective-permute-start(f32[2,4,2048]{2,1,0:T(4,128)S(1)} %bitcast.256), channel_id=1, source_target_pairs={{0,128},{32,160},{64,192},{96,224},{128,0},{160,32},{192,64},{224,... | collective-permute-start | bytes 196616 | tf_op jit(solution)/shard_map/ppermute | solution.py:12
  65.7 4.2 %collective-permute-done.4 = f32[2,4,2048]{2,1,0:T(4,128)S(1)} collective-permute-done((f32[2,4,2048]{2,1,0:T(4,128)S(1)}, f32[2,4,2048]{2,1,0:T(4,128)S(1)}, u32[]{:S(2)}, u32[]{:S(2)}) %collective-permute-start.4) | collective-permute-done | bytes 65568 | tf_op jit(solution)/shard_map/ppermute | solution.py:12
  70.0 0.5 dynamic_update_slice.22
  70.8 1.9 %collective-permute-start.5 = (f32[2,2,4096]{2,1,0:T(2,128)S(1)}, f32[2,2,4096]{2,1,0:T(2,128)S(1)}, u32[]{:S(2)}, u32[]{:S(2)}) collective-permute-start(f32[2,2,4096]{2,1,0:T(2,128)S(1)} %bitcast.253), channel_id=1, source_target_pairs={{0,256},{32,288},{64,320},{96,352},{128,384},{160,416},{192,448},{... | collective-permute-start | bytes 196616 | tf_op jit(solution)/shard_map/ppermute | solution.py:12
  72.7 5.3 %collective-permute-done.5 = f32[2,2,4096]{2,1,0:T(2,128)S(1)} collective-permute-done((f32[2,2,4096]{2,1,0:T(2,128)S(1)}, f32[2,2,4096]{2,1,0:T(2,128)S(1)}, u32[]{:S(2)}, u32[]{:S(2)}) %collective-permute-start.5) | collective-permute-done | bytes 65568 | tf_op jit(solution)/shard_map/ppermute | solution.py:12
  78.0 0.5 dynamic_update_slice.23
  78.8 5.0 %collective-permute-start.6 = (f32[2,1,8192]{2,1,0:T(1,128)S(1)}, f32[2,1,8192]{2,1,0:T(1,128)S(1)}, u32[]{:S(2)}, u32[]{:S(2)}) collective-permute-start(f32[2,1,8192]{2,1,0:T(1,128)S(1)} %dynamic-slice_bitcast_fusion), channel_id=1, source_target_pairs={{0,512},{32,544},{64,576},{96,608},{128,640},{160,672},{192,704},{... | collective-permute-start | bytes 196616 | tf_op jit(solution)/shard_map/ppermute | solution.py:12
  83.8 5.1 %collective-permute-done.6 = f32[2,1,8192]{2,1,0:T(1,128)S(1)} collective-permute-done((f32[2,1,8192]{2,1,0:T(1,128)S(1)}, f32[2,1,8192]{2,1,0:T(1,128)S(1)}, u32[]{:S(2)}, u32[]{:S(2)}) %collective-permute-start.6) | collective-permute-done | bytes 65568 | tf_op jit(solution)/shard_map/ppermute | solution.py:12
  88.9 0.7 dynamic_update_slice.24
  90.5 0.3 fusion.40
  91.4 0.3 fusion.5
  91.7 0.3 fusion.34
  92.0 0.3 fusion.38
  92.3 0.3 fusion.4
  92.6 0.3 convolution_subtract_fusion.3
  93.2 0.3 fusion.32
  93.5 0.3 convolution_add_fusion.3
  93.7 0.3 fusion.3
  94.0 0.3 fusion.22
  94.3 0.3 fusion.26
  94.6 0.3 fusion.2
  94.9 0.3 convolution_subtract_fusion.1
  95.2 0.3 fusion.20
  95.5 0.3 fusion.16
  95.8 0.3 convolution_add_fusion.1
  96.1 0.3 fusion.1
  96.5 0.3 fusion
  96.9 0.8 pad_maximum_fusion
  (56 shorter events, 4.8 us)
Async XLA Ops:
  0.0 8.2 %copy-start = (f32[10,2,128,128]{3,2,1,0:T(8,128)S(1)}, f32[10,2,128,128]{3,2,1,0:T(8,128)}, u32[]{:S(2)}) copy-start(f32[10,2,128,128]{3,2,1,0:T(8,128)} %param.8) | copy-start | bytes 3932164
  0.0 8.2 %copy-start.1 = (f32[128]{0:T(128)S(1)}, f32[128]{0:T(128)}, u32[]{:S(2)}) copy-start(f32[128]{0:T(128)} %param.9) | copy-start | bytes 1540
  4.3 7.1 %copy-start.2 = (s32[2]{0:T(128)S(1)}, s32[2]{0:T(128)}, u32[]{:S(2)}) copy-start(s32[2]{0:T(128)} %param.12) | copy-start | bytes 28
  10.0 8.8 %copy-start.3 = (s32[4]{0:T(128)S(1)}, s32[4]{0:T(128)}, u32[]{:S(2)}) copy-start(s32[4]{0:T(128)} %param.13) | copy-start | bytes 52
  16.8 5.5 %collective-permute-start = (f32[2,1,4,2048]{3,0,2,1:T(2,128)S(1)}, f32[2,1,4,2048]{3,0,2,1:T(2,128)S(1)}, u32[]{:S(2)}, u32[]{:S(2)}) collective-permute-start(f32[2,1,4,2048]{3,0,2,1:T(2,128)S(1)} %bitcast_select_fusion), channel_id=1, source_target_pairs={{0,2},{2,0},{4,6},{6,4},{8,10},{10,8},{12,14},{14,12},{16,18},{18,... | collective-permute-start | bytes 196616 | tf_op jit(solution)/shard_map/ppermute | solution.py:12
  24.6 19.2 %collective-permute-start.1 = (f32[2,32,4,64]{3,1,0,2:T(8,128)S(1)}, f32[2,32,4,64]{3,1,0,2:T(8,128)S(1)}, u32[]{:S(2)}, u32[]{:S(2)}) collective-permute-start(f32[2,32,4,64]{3,1,0,2:T(8,128)S(1)} %select_bitcast_fusion), channel_id=1, source_target_pairs={{0,1},{1,0},{2,3},{3,2},{4,5},{5,4},{6,7},{7,6},{8,9},{9,8},{10,11... | collective-permute-start | bytes 196616 | tf_op jit(solution)/shard_map/ppermute | solution.py:12
  44.9 7.1 %collective-permute-start.2 = (f32[2,16,512]{2,1,0:T(8,128)S(1)}, f32[2,16,512]{2,1,0:T(8,128)S(1)}, u32[]{:S(2)}, u32[]{:S(2)}) collective-permute-start(f32[2,16,512]{2,1,0:T(8,128)S(1)} %bitcast.255), channel_id=1, source_target_pairs={{0,32},{32,0},{64,96},{96,64},{128,160},{160,128},{192,224},{224,1... | collective-permute-start | bytes 196616 | tf_op jit(solution)/shard_map/ppermute | solution.py:12
  52.9 10.1 %collective-permute-start.3 = (f32[2,8,1024]{2,1,0:T(8,128)S(1)}, f32[2,8,1024]{2,1,0:T(8,128)S(1)}, u32[]{:S(2)}, u32[]{:S(2)}) collective-permute-start(f32[2,8,1024]{2,1,0:T(8,128)S(1)} %bitcast.254), channel_id=1, source_target_pairs={{0,64},{32,96},{64,0},{96,32},{128,192},{160,224},{192,128},{224,1... | collective-permute-start | bytes 196616 | tf_op jit(solution)/shard_map/ppermute | solution.py:12
  63.8 6.2 %collective-permute-start.4 = (f32[2,4,2048]{2,1,0:T(4,128)S(1)}, f32[2,4,2048]{2,1,0:T(4,128)S(1)}, u32[]{:S(2)}, u32[]{:S(2)}) collective-permute-start(f32[2,4,2048]{2,1,0:T(4,128)S(1)} %bitcast.256), channel_id=1, source_target_pairs={{0,128},{32,160},{64,192},{96,224},{128,0},{160,32},{192,64},{224,... | collective-permute-start | bytes 196616 | tf_op jit(solution)/shard_map/ppermute | solution.py:12
  70.8 7.2 %collective-permute-start.5 = (f32[2,2,4096]{2,1,0:T(2,128)S(1)}, f32[2,2,4096]{2,1,0:T(2,128)S(1)}, u32[]{:S(2)}, u32[]{:S(2)}) collective-permute-start(f32[2,2,4096]{2,1,0:T(2,128)S(1)} %bitcast.253), channel_id=1, source_target_pairs={{0,256},{32,288},{64,320},{96,352},{128,384},{160,416},{192,448},{... | collective-permute-start | bytes 196616 | tf_op jit(solution)/shard_map/ppermute | solution.py:12
  78.8 10.1 %collective-permute-start.6 = (f32[2,1,8192]{2,1,0:T(1,128)S(1)}, f32[2,1,8192]{2,1,0:T(1,128)S(1)}, u32[]{:S(2)}, u32[]{:S(2)}) collective-permute-start(f32[2,1,8192]{2,1,0:T(1,128)S(1)} %dynamic-slice_bitcast_fusion), channel_id=1, source_target_pairs={{0,512},{32,544},{64,576},{96,608},{128,640},{160,672},{192,704},{... | collective-permute-start | bytes 196616 | tf_op jit(solution)/shard_map/ppermute | solution.py:12
where the time goes:
time: 98.3 us; the launch traced here: 97.7 us
  waiting for transfers between devices  32 us (33%)
  starting transfers between devices  29.7 us (30%)
  matrix products  16.7 us (17%)
  local copies, waits for them, and re-layouts  9.93 us (10%)
  between operations  5.04 us (5%)
  other arithmetic  4.4 us (4%)
    ppermute x7, waiting for transfers between devices, partner(): return lax.ppermute(value, axis, pairs)  32 us
    ppermute x7, starting transfers between devices, partner(): return lax.ppermute(value, axis, pairs)  29.7 us
    dot_general x20, matrix products, product(): return jnp.einsum('...b,ab->...a', values, matrix, precision=HIGH)  8.93 us
    dot_general x20, matrix products, product(): return jnp.einsum('ab,rbc->rac', matrix, values, precision=HIGH)  7.74 us
    dynamic_update_slice x5, local copies, waits for them, and re-layouts, on_device(): shaped = lax.dynamic_update_index_in_dim(shaped, received, 1 - own_bit, 2)  2.78 us
  transfers between devices with their start and end apart: 7, of which 6 were waited for; matrix products, arithmetic and copies ran while one was open for 2% of the time, Pallas kernels for 0%

commit v1 on v0

v1 whole, which is shorter than its diff:
```python
import jax
import jax.numpy as jnp
from jax import lax
from jax.experimental import pallas as pl
from jax.experimental.pallas import tpu as pltpu
from jax.sharding import PartitionSpec as P

MESH = pl.DeviceIdType.MESH
F32 = jnp.float32
BF16 = jnp.bfloat16
I32 = jnp.int32
NN = (((1,), (0,)), ((), ()))
NT = (((1,), (1,)), ((), ()))
G = 128


def dot(x, w, dims=NN):
    return lax.dot_general(x, w, dims, preferred_element_type=F32)


def split(x):
    high = x.astype(BF16)
    return high, (x - high.astype(F32)).astype(BF16)


def dot3(x, w, dims=NN):
    rows = x[0].shape[0]
    both = dot(jnp.concatenate(x, axis=0), w[0], dims)
    return both[:rows] + both[rows:] + dot(x[0], w[1], dims)


def beside(left, right):
    return jnp.concatenate([left, right], axis=1)


def above(top, bottom):
    return jnp.concatenate([top, bottom], axis=0)


def complex_split(real, imag):
    real_high, real_low = split(real)
    imag_high, imag_low = split(imag)
    return (real_high, imag_high), (real_low, imag_low)


def left_form(pieces):
    return tuple(beside(real, imag) for real, imag in pieces)


def right_form(pieces):
    return tuple(above(beside(real, imag), beside(-imag, real)) for real, imag in pieces)


def row_form(pieces):
    return tuple(above(beside(real, -imag), beside(imag, real)) for real, imag in pieces)


def complex_product(left, right):
    out = dot3(left_form(left), right_form(right))
    return complex_split(out[:, :G], out[:, G:])


def fields_one(index):
    return index >> 6, (index >> 4) & 3, (index >> 3) & 1, index & 7


def fields_two(index):
    return (index >> 3) & 1, (index >> 1) & 3, index & 1, index >> 4


def exchange_lane(first, second, lane, low_bound, high_bound):
    rolled_first = pltpu.roll(first, G // 2, axis=1)
    rolled_second = pltpu.roll(second, G // 2, axis=1)
    return (
        jnp.where(lane < low_bound, first, rolled_second),
        jnp.where(lane >= high_bound, second, rolled_first),
    )


def tiles_two(value):
    shaped = value.reshape(8, 2, 8, G)
    return shaped[:, 0].reshape(64, G), shaped[:, 1].reshape(64, G)


def join_two(first, second):
    shaped = jnp.stack([first.reshape(8, 8, G), second.reshape(8, 8, G)], axis=1)
    return shaped.reshape(G, G)


def kernel(
    state_ref,
    gates_ref,
    low_ref,
    mid_ref,
    top_ref,
    swap_ref,
    order_ref,
    out_ref,
    gate,
    vector,
    keep,
    give,
    gift,
    send_one,
    land_one,
    send_two,
    land_two,
    back_left,
    back_right,
    load_sem,
    gift_send,
    gift_recv,
    send_sem,
    recv_sem,
):
    wide = lax.axis_index("wide")
    mid = lax.axis_index("mid")
    low = lax.axis_index("low")
    depth = wide // 4
    across = lax.rem(wide, 4)
    core = lax.rem(mid, 2)
    place_x = low * 4 + across

    def x_peer(slot):
        return (depth * 4 + lax.rem(slot, 4), mid, slot // 4)

    def z_peer(slot):
        return (slot * 4 + across, mid, low)

    partner = (wide, mid + 1 - 2 * core, low)

    barrier = pltpu.get_barrier_semaphore()
    for step in range(1, 8):
        pl.semaphore_signal(
            barrier, inc=1, device_id=x_peer(lax.rem(place_x + step, 8)), device_id_type=MESH
        )
        pl.semaphore_signal(
            barrier, inc=1, device_id=z_peer(lax.rem(depth + step, 8)), device_id_type=MESH
        )
    pl.semaphore_signal(barrier, inc=1, device_id=partner, device_id_type=MESH)

    first_gates = pltpu.make_async_copy(
        gates_ref.at[pl.ds(0, 4)], gate.at[pl.ds(0, 4)], load_sem.at[0]
    )
    first_gates.start()
    load_state = pltpu.make_async_copy(state_ref, vector, load_sem.at[1])
    load_state.start()
    last_gates = pltpu.make_async_copy(
        gates_ref.at[pl.ds(4, 6)], gate.at[pl.ds(4, 6)], load_sem.at[2]
    )
    last_gates.start()

    first_swap = swap_ref[0]
    second_swap = swap_ref[1]
    low_bound = jnp.where(second_swap == 0, G // 2, G)
    high_bound = jnp.where(second_swap == 0, G // 2, 0)
    lane = lax.broadcasted_iota(I32, (64, G), 1)

    swapped = first_swap + 1
    weights = []
    holds = []
    for place in range(4):
        source = order_ref[place]
        is_swapped = source == swapped
        weights.append(jnp.where(is_swapped, 0, jnp.left_shift(8, source)))
        holds.append(jnp.where(is_swapped, 1, 0))
    low_weight = jnp.where(second_swap == 2, 2, 1)
    spare_weight = 3 - low_weight
    swapped_weight = jnp.left_shift(8, swapped)
    keep_shift = core * swapped_weight
    give_shift = (1 - core) * swapped_weight
    row = lax.broadcasted_iota(I32, (G, G), 0)
    column = lax.broadcasted_iota(I32, (G, G), 1)

    def front_rows(fields):
        low_bit, x_hi, spare, z = fields
        bits = (x_hi >> 1, z & 1, (z >> 1) & 1, z >> 2)
        source = low_bit * low_weight + spare * spare_weight + (x_hi & 1) * 4
        held = jnp.zeros_like(source)
        for bit, weight, hold in zip(bits, weights, holds):
            source = source + bit * weight
            held = held + bit * hold
        return jnp.where(held == core, source, -G)

    def pick(rows, shift):
        return jnp.where(rows + shift == column, 1.0, 0.0).astype(BF16)

    rows_one = front_rows(fields_one(row))
    rows_two = front_rows(fields_two(row))
    picks = jnp.concatenate(
        [
            pick(rows_one, keep_shift),
            pick(rows_two, keep_shift),
            pick(rows_one, give_shift),
            pick(rows_two, give_shift),
        ],
        axis=0,
    )

    low_angle = low_ref[...] + top_ref[0, 0]
    mid_angle = mid_ref[...]
    low_cos, low_sin = jnp.cos(low_angle), jnp.sin(low_angle)
    mid_cos, mid_sin = jnp.cos(mid_angle), jnp.sin(mid_angle)

    def turned(number, cosine, sine):
        real, imag = gate[number, 0], gate[number, 1]
        return complex_split(real * cosine - imag * sine, real * sine + imag * cosine)

    first_gates.wait()
    inner = complex_product(
        turned(2, low_cos, low_sin), complex_split(gate[0, 0], gate[0, 1])
    )
    (three_high, three_low) = complex_split(gate[3, 0], gate[3, 1])
    picked = (
        dot(picks, beside(*three_high)).astype(BF16),
        dot(picks, beside(*three_low)).astype(BF16),
    )
    outer = dot3(picked, right_form(turned(1, mid_cos, mid_sin)))
    real_part, imag_part = outer[:, :G], outer[:, G:]
    outer = jnp.concatenate(
        [
            beside(real_part[:G], -imag_part[:G]),
            beside(imag_part[G : 2 * G], real_part[G : 2 * G]),
            beside(real_part[2 * G : 3 * G], -imag_part[2 * G : 3 * G]),
            beside(imag_part[3 * G :], real_part[3 * G :]),
        ],
        axis=0,
    )
    load_state.wait()
    turned_state = dot3(
        left_form(complex_split(vector[0], vector[1])), row_form(inner), NT
    )
    stacked = above(turned_state[:, :G], turned_state[:, G:])
    front = dot3(split(outer), split(stacked))
    keep[0] = front[:G]
    keep[1] = front[G : 2 * G]
    give[0] = front[2 * G : 3 * G]
    give[1] = front[3 * G :]

    pl.semaphore_wait(barrier, 15)

    gifts = []
    for part in range(2):
        copy = pltpu.make_async_remote_copy(
            src_ref=give.at[part],
            dst_ref=gift.at[part],
            send_sem=gift_send.at[part],
            recv_sem=gift_recv.at[part],
            device_id=partner,
            device_id_type=MESH,
        )
        copy.start()
        gifts.append(copy)

    def block(slot):
        return pl.ds(pl.multiple_of(slot * 16, 16), 16)

    def spread(stage, part, source, target, mine, peer):
        copies = []
        for step in (4, 3, 5, 2, 6, 1, 7):
            slot = lax.rem(mine + step, 8)
            copy = pltpu.make_async_remote_copy(
                src_ref=source.at[part, block(slot), :],
                dst_ref=target.at[part, block(mine), :],
                send_sem=send_sem.at[stage, part, step],
                recv_sem=recv_sem.at[stage, part, step],
                device_id=peer(slot),
                device_id_type=MESH,
            )
            copy.start()
            copies.append(copy)
        target[part, block(mine), :] = source[part, block(mine), :]
        return copies

    gifts[0].wait_recv()
    real_part = keep[0] + gift[0]
    first, second = exchange_lane(real_part[:64], real_part[64:], lane, low_bound, high_bound)
    send_one[0, :64] = first
    send_one[0, 64:] = second
    copies_real = spread(0, 0, send_one, land_one, place_x, x_peer)
    gifts[1].wait_recv()
    imag_part = keep[1] + gift[1]
    first, second = tiles_two(imag_part)
    first, second = exchange_lane(first, second, lane, low_bound, high_bound)
    send_one[1] = join_two(first, second)
    copies_imag = spread(0, 1, send_one, land_one, depth, z_peer)

    last_gates.wait()

    def pieces(number):
        return complex_split(gate[number, 0], gate[number, 1])

    inner = complex_product(pieces(8), complex_product(pieces(6), pieces(4)))
    for level, value in enumerate(row_form(inner)):
        back_right[level] = value

    def natural(fields):
        low_bit, x_hi, spare, z = fields
        return low_bit * low_weight + spare * spare_weight + x_hi * 4 + z * 16

    order = beside(
        jnp.where(natural(fields_two(column)) == row, 1.0, 0.0).astype(BF16),
        jnp.where(natural(fields_one(column)) == row, 1.0, 0.0).astype(BF16),
    )
    outer = complex_product(pieces(9), complex_product(pieces(7), pieces(5)))
    for level, (real, imag) in enumerate(outer):
        real = dot(real, order).astype(BF16)
        imag = dot(imag, order).astype(BF16)
        back_left[level] = above(
            beside(real[:, :G], -imag[:, G:]), beside(imag[:, :G], real[:, G:])
        )

    for copy in copies_real:
        copy.wait_recv()
    for slot in range(8):
        for low_bit in range(2):
            send_two[0, slot * 16 + low_bit * 8 : slot * 16 + low_bit * 8 + 8, :] = land_one[
                0, pl.ds(low_bit * 64 + slot, 8, stride=8), :
            ]
    more_real = spread(1, 0, send_two, land_two, depth, z_peer)
    for copy in copies_imag:
        copy.wait_recv()
    for slot in range(8):
        for spare in range(2):
            start = (slot // 4) * 8 + (slot % 4) * 2 + spare
            send_two[1, slot * 16 + spare * 8 : slot * 16 + spare * 8 + 8, :] = land_one[
                1, pl.ds(start, 8, stride=16), :
            ]
    more_imag = spread(1, 1, send_two, land_two, place_x, x_peer)

    for copy in more_real + more_imag:
        copy.wait_recv()
    first, second = tiles_two(land_two[0])
    first, second = exchange_lane(first, second, lane, low_bound, high_bound)
    real_part = join_two(first, second)
    imag_part = land_two[1]
    first, second = exchange_lane(imag_part[:64], imag_part[64:], lane, low_bound, high_bound)
    stacked = jnp.concatenate([real_part, first, second], axis=0)
    middle = dot3((back_left[0], back_left[1]), split(stacked))
    result = dot3(
        left_form(complex_split(middle[:G], middle[G:])), (back_right[0], back_right[1]), NT
    )
    out_ref[0] = result[:, :G]
    out_ref[1] = result[:, G:]
    for copy in gifts + copies_real + copies_imag + more_real + more_imag:
        copy.wait_send()


def on_device(state, gates, phase_low, phase_mid, phase_top, swap_qubits, regroup_order):
    square = (2, G, G)
    space = pltpu.VMEM
    out = pl.pallas_call(
        kernel,
        out_shape=jax.ShapeDtypeStruct(square, F32),
        in_specs=[
            pl.BlockSpec(memory_space=pl.ANY),
            pl.BlockSpec(memory_space=pl.ANY),
            pl.BlockSpec(memory_space=space),
            pl.BlockSpec(memory_space=space),
            pl.BlockSpec(memory_space=pltpu.SMEM),
            pl.BlockSpec(memory_space=pltpu.SMEM),
            pl.BlockSpec(memory_space=pltpu.SMEM),
        ],
        out_specs=pl.BlockSpec(memory_space=space),
        scratch_shapes=[
            pltpu.VMEM(gates.shape, F32),
            pltpu.VMEM(square, F32),
            pltpu.VMEM(square, F32),
            pltpu.VMEM(square, F32),
            pltpu.VMEM(square, F32),
            pltpu.VMEM(square, F32),
            pltpu.VMEM(square, F32),
            pltpu.VMEM(square, F32),
            pltpu.VMEM(square, F32),
            pltpu.VMEM((2, 2 * G, 2 * G), BF16),
            pltpu.VMEM((2, 2 * G, 2 * G), BF16),
            pltpu.SemaphoreType.DMA((3,)),
            pltpu.SemaphoreType.DMA((2,)),
            pltpu.SemaphoreType.DMA((2,)),
            pltpu.SemaphoreType.DMA((2, 2, 8)),
            pltpu.SemaphoreType.DMA((2, 2, 8)),
        ],
        compiler_params=pltpu.CompilerParams(collective_id=0, has_side_effects=True),
    )(
        state.reshape(square),
        gates,
        phase_low.reshape(1, G),
        phase_mid.reshape(1, G),
        phase_top.reshape(1, 1),
        swap_qubits,
        regroup_order,
    )
    return out.reshape(state.shape)


def solution(mesh):
    return jax.shard_map(
        on_device,
        mesh=mesh,
        in_specs=(
            P(None, "wide", "mid", "low", None),
            P(),
            P(),
            P(),
            P("wide", "mid", "low", None),
            P(),
            P(),
        ),
        out_specs=P(None, "wide", "mid", "low", None),
        check_vma=False,
    )
```

time: 98.3 us -> 35.8 us (0.36)
  the two profiles are of different devices: /device:TPU:2 before, /device:TPU:1 now
where the time goes in v1:
time: 35.8 us; the launch traced here: 35.6 us
  Pallas kernels  33.4 us (93%)
  local copies, waits for them, and re-layouts  1.57 us (4%)
  between operations  0.66 us (2%)
    pallas_call x1, Pallas kernels, on_device(): pl.pallas_call(kernel, out_shape=jax.ShapeDtypeStruct(square, F32), in_sp...  33.4 us
    unnamed x1, local copies, waits for them, and re-layouts  1.57 us

profile of v1, /device:TPU:1, one launch (start us, length us, event | category | flops | bytes accessed | tf_op | source)
XLA Modules:
  0.0 35.6 jit_solution(2972514352255765972)
XLA Ops:
  0.7 33.4 %shard_map.73 = f32[2,128,128]{2,1,0:T(8,128)} custom-call(f32[2,128,128]{2,1,0:T(8,128)} %bitcast.7, f32[10,2,128,128]{3,2,1,0:T(8,128)} %gates_ref.1, f32[1,128]{1,0:T(1,128)} %bitcast.8, f32[1,128]{1,0:T(1,128)} %bitcast.9, f32[1,1]{1,0:T(1,128)} %bitcast.5.top_ref, s32[2]{0:T(128)} %swap_ref.1, s32[4]{0:T(128)} %order_ref.1), custom_call_target="tpu_custom_call" | custom-call | tf_op jit(solution)/shard_map/pallas_call | solution.py:352
  34.1 1.6 %copy.11 = f32[2,1,1,1,16384]{4,3,2,1,0:T(1,128)} copy(f32[2,1,1,1,16384]{4,3,2,1,0:T(1,128)} %bitcast.6) | data formatting | bytes 262144

commit v2 on v1

--- a/solution.py
+++ b/solution.py
@@ -87,15 +87,18 @@
     return shaped.reshape(G, G)
 
 
-def kernel(
+def travel_kernel(
     state_ref,
     gates_ref,
     low_ref,
     mid_ref,
     top_ref,
-    swap_ref,
-    order_ref,
-    out_ref,
+    swap_hbm,
+    order_hbm,
+    land_two,
+    back_left,
+    back_right,
+    masks,
     gate,
     vector,
     keep,
@@ -104,9 +107,10 @@
     send_one,
     land_one,
     send_two,
-    land_two,
-    back_left,
-    back_right,
+    angles,
+    top_value,
+    swap_ref,
+    order_ref,
     load_sem,
     gift_send,
     gift_recv,
@@ -129,6 +133,22 @@
 
     partner = (wide, mid + 1 - 2 * core, low)
 
+    def load(source, target, number):
+        copy = pltpu.make_async_copy(source, target, load_sem.at[number])
+        copy.start()
+        return copy
+
+    small = [
+        load(swap_hbm, swap_ref, 3),
+        load(order_hbm, order_ref, 4),
+        load(low_ref, angles.at[pl.ds(0, 1)], 5),
+        load(mid_ref, angles.at[pl.ds(1, 1)], 6),
+        load(top_ref, top_value, 7),
+    ]
+    first_gates = load(gates_ref.at[pl.ds(0, 4)], gate.at[pl.ds(0, 4)], 0)
+    load_state = load(state_ref, vector, 1)
+    last_gates = load(gates_ref.at[pl.ds(4, 6)], gate.at[pl.ds(4, 6)], 2)
+
     barrier = pltpu.get_barrier_semaphore()
     for step in range(1, 8):
         pl.semaphore_signal(
@@ -139,22 +159,16 @@
         )
     pl.semaphore_signal(barrier, inc=1, device_id=partner, device_id_type=MESH)
 
-    first_gates = pltpu.make_async_copy(
-        gates_ref.at[pl.ds(0, 4)], gate.at[pl.ds(0, 4)], load_sem.at[0]
-    )
-    first_gates.start()
-    load_state = pltpu.make_async_copy(state_ref, vector, load_sem.at[1])
-    load_state.start()
-    last_gates = pltpu.make_async_copy(
-        gates_ref.at[pl.ds(4, 6)], gate.at[pl.ds(4, 6)], load_sem.at[2]
-    )
-    last_gates.start()
-
+    for copy in small:
+        copy.wait()
     first_swap = swap_ref[0]
     second_swap = swap_ref[1]
     low_bound = jnp.where(second_swap == 0, G // 2, G)
     high_bound = jnp.where(second_swap == 0, G // 2, 0)
     lane = lax.broadcasted_iota(I32, (64, G), 1)
+    short_lane = lax.broadcasted_iota(I32, (8, G), 1)
+    masks[0] = jnp.where(short_lane < low_bound, 1, 0)
+    masks[1] = jnp.where(short_lane >= high_bound, 1, 0)
 
     swapped = first_swap + 1
     weights = []
@@ -197,10 +211,12 @@
         axis=0,
     )
 
-    low_angle = low_ref[...] + top_ref[0, 0]
-    mid_angle = mid_ref[...]
-    low_cos, low_sin = jnp.cos(low_angle), jnp.sin(low_angle)
-    mid_cos, mid_sin = jnp.cos(mid_angle), jnp.sin(mid_angle)
+    angle = angles[...]
+    is_low = lax.broadcasted_iota(I32, (2, G), 0) == 0
+    angle = angle + jnp.where(is_low, top_value[0, 0, 0, 0], 0.0)
+    cosines, sines = jnp.cos(angle), jnp.sin(angle)
+    low_cos, low_sin = cosines[0:1], sines[0:1]
+    mid_cos, mid_sin = cosines[1:2], sines[1:2]
 
     def turned(number, cosine, sine):
         real, imag = gate[number, 0], gate[number, 1]
@@ -215,23 +231,25 @@
         dot(picks, beside(*three_high)).astype(BF16),
         dot(picks, beside(*three_low)).astype(BF16),
     )
-    outer = dot3(picked, right_form(turned(1, mid_cos, mid_sin)))
-    real_part, imag_part = outer[:, :G], outer[:, G:]
-    outer = jnp.concatenate(
-        [
-            beside(real_part[:G], -imag_part[:G]),
-            beside(imag_part[G : 2 * G], real_part[G : 2 * G]),
-            beside(real_part[2 * G : 3 * G], -imag_part[2 * G : 3 * G]),
-            beside(imag_part[3 * G :], real_part[3 * G :]),
-        ],
-        axis=0,
+    picked = tuple(
+        jnp.concatenate(
+            [
+                beside(rows[:G, :G], -rows[:G, G:]),
+                beside(rows[G : 2 * G, G:], rows[G : 2 * G, :G]),
+                beside(rows[2 * G : 3 * G, :G], -rows[2 * G : 3 * G, G:]),
+                beside(rows[3 * G :, G:], rows[3 * G :, :G]),
+            ],
+            axis=0,
+        )
+        for rows in picked
     )
     load_state.wait()
-    turned_state = dot3(
-        left_form(complex_split(vector[0], vector[1])), row_form(inner), NT
-    )
-    stacked = above(turned_state[:, :G], turned_state[:, G:])
-    front = dot3(split(outer), split(stacked))
+    value = dot3(
+        row_form(turned(1, mid_cos, mid_sin)), split(above(vector[0], vector[1]))
+    )
+    value = dot3(left_form(complex_split(value[:G], value[G:])), row_form(inner), NT)
+    stacked = above(value[:, :G], value[:, G:])
+    front = dot3(picked, split(stacked))
     keep[0] = front[:G]
     keep[1] = front[G : 2 * G]
     give[0] = front[2 * G : 3 * G]
@@ -330,11 +348,25 @@
 
     for copy in more_real + more_imag:
         copy.wait_recv()
-    first, second = tiles_two(land_two[0])
-    first, second = exchange_lane(first, second, lane, low_bound, high_bound)
-    real_part = join_two(first, second)
-    imag_part = land_two[1]
-    first, second = exchange_lane(imag_part[:64], imag_part[64:], lane, low_bound, high_bound)
+    for copy in gifts + copies_real + copies_imag + more_real + more_imag:
+        copy.wait_send()
+
+
+def final_kernel(landed, back_left, back_right, masks, out_ref):
+    keep_first = jnp.concatenate([masks[0]] * 8, axis=0) > 0
+    keep_second = jnp.concatenate([masks[1]] * 8, axis=0) > 0
+
+    def exchange(first, second):
+        rolled_first = pltpu.roll(first, G // 2, axis=1)
+        rolled_second = pltpu.roll(second, G // 2, axis=1)
+        return (
+            jnp.where(keep_first, first, rolled_second),
+            jnp.where(keep_second, second, rolled_first),
+        )
+
+    real_part = join_two(*exchange(*tiles_two(landed[0])))
+    imag_part = landed[1]
+    first, second = exchange(imag_part[:64], imag_part[64:])
     stacked = jnp.concatenate([real_part, first, second], axis=0)
     middle = dot3((back_left[0], back_left[1]), split(stacked))
     result = dot3(
@@ -342,39 +374,31 @@
     )
     out_ref[0] = result[:, :G]
     out_ref[1] = result[:, G:]
-    for copy in gifts + copies_real + copies_imag + more_real + more_imag:
-        copy.wait_send()
 
 
 def on_device(state, gates, phase_low, phase_mid, phase_top, swap_qubits, regroup_order):
     square = (2, G, G)
-    space = pltpu.VMEM
-    out = pl.pallas_call(
-        kernel,
-        out_shape=jax.ShapeDtypeStruct(square, F32),
-        in_specs=[
-            pl.BlockSpec(memory_space=pl.ANY),
-            pl.BlockSpec(memory_space=pl.ANY),
-            pl.BlockSpec(memory_space=space),
-            pl.BlockSpec(memory_space=space),
-            pl.BlockSpec(memory_space=pltpu.SMEM),
-            pl.BlockSpec(memory_space=pltpu.SMEM),
-            pl.BlockSpec(memory_space=pltpu.SMEM),
-        ],
-        out_specs=pl.BlockSpec(memory_space=space),
+    doubled = (2, 2 * G, 2 * G)
+    vmem = pl.BlockSpec(memory_space=pltpu.VMEM)
+    hbm = pl.BlockSpec(memory_space=pltpu.HBM)
+    between = pl.pallas_call(
+        travel_kernel,
+        out_shape=(
+            pltpu.VMEM(square, F32),
+            pltpu.VMEM(doubled, BF16),
+            pltpu.VMEM(doubled, BF16),
+            pltpu.VMEM((2, 8, G), I32),
+        ),
+        in_specs=[hbm] * 7,
+        out_specs=(vmem,) * 4,
         scratch_shapes=[
             pltpu.VMEM(gates.shape, F32),
-            pltpu.VMEM(square, F32),
-            pltpu.VMEM(square, F32),
-            pltpu.VMEM(square, F32),
-            pltpu.VMEM(square, F32),
-            pltpu.VMEM(square, F32),
-            pltpu.VMEM(square, F32),
-            pltpu.VMEM(square, F32),
-            pltpu.VMEM(square, F32),
-            pltpu.VMEM((2, 2 * G, 2 * G), BF16),
-            pltpu.VMEM((2, 2 * G, 2 * G), BF16),
-            pltpu.SemaphoreType.DMA((3,)),
+            *[pltpu.VMEM(square, F32)] * 7,
+            pltpu.VMEM((2, G), F32),
+            pltpu.SMEM((1, 1, 1, 1), F32),
+            pltpu.SMEM((2,), I32),
+            pltpu.SMEM((4,), I32),
+            pltpu.SemaphoreType.DMA((8,)),
             pltpu.SemaphoreType.DMA((2,)),
             pltpu.SemaphoreType.DMA((2,)),
             pltpu.SemaphoreType.DMA((2, 2, 8)),
@@ -386,10 +410,17 @@
         gates,
         phase_low.reshape(1, G),
         phase_mid.reshape(1, G),
-        phase_top.reshape(1, 1),
+        phase_top,
         swap_qubits,
         regroup_order,
     )
+    out = pl.pallas_call(
+        final_kernel,
+        out_shape=jax.ShapeDtypeStruct(square, F32),
+        in_specs=[vmem] * 4,
+        out_specs=vmem,
+        compiler_params=pltpu.CompilerParams(vmem_limit_bytes=8 << 20),
+    )(*between)
     return out.reshape(state.shape)
 
 

time: 35.8 us -> 33.4 us (0.933)
  local copies, waits for them, and re-layouts: 1.57 us -> 0 us
  Pallas kernels: 33.4 us -> 32.6 us
    unnamed x1 -> x0, local copies, waits for them, and re-layouts: 1.57 us -> none
    pallas_call x1 -> x2, Pallas kernels: 33.4 us -> 32.6 us  [the longest x1 31.4 us: on_device(): pl.pallas_call(travel_kernel, out_shape=(pltpu.VMEM(square, F32), pltpu.V...]
where the time goes in v2:
time: 33.4 us; the launch traced here: 33.3 us
  Pallas kernels  32.6 us (98%)
  between operations  0.66 us (2%)
    pallas_call x1, Pallas kernels, on_device(): pl.pallas_call(travel_kernel, out_shape=(pltpu.VMEM(square, F32), pltpu.V...  31.4 us
    pallas_call x1, Pallas kernels, on_device(): pl.pallas_call(final_kernel, out_shape=jax.ShapeDtypeStruct(square, F32),...  1.21 us

profile of v2, /device:TPU:1, one launch (start us, length us, event | category | flops | bytes accessed | tf_op | source)
XLA Modules:
  0.0 33.3 jit_solution(2367088000919340652)
XLA Ops:
  0.7 31.4 %shard_map.73 = (f32[2,128,128]{2,1,0:T(8,128)S(1)}, bf16[2,256,256]{2,1,0:T(8,128)(2,1)S(1)}, bf16[2,256,256]{2,1,0:T(8,128)(2,1)S(1)}, s32[2,8,128]{2,1,0:T(8,128)S(1)}) custom-call(f32[2,128,128]{2,1,0:T(8,128)} %bitcast.4, f32[10,2,128,128]{3,2,1,0:T(8,128)} %gates_ref.1, f32[1,128]{1,0:T(1,128)} %bitcast.5, f32[1,128]{1,0:T(1,128)} %bitcast.6, ...), custom_call_target="tpu_custom_call" | custom-call | tf_op jit(solution)/shard_map/pallas_call | solution.py:384
  32.1 1.2 %shard_map.74 = f32[2,128,128]{2,1,0:T(8,128)} custom-call(f32[2,128,128]{2,1,0:T(8,128)S(1)} %get-tuple-element.9.landed, bf16[2,256,256]{2,1,0:T(8,128)(2,1)S(1)} %get-tuple-element.10.back_left, bf16[2,256,256]{2,1,0:T(8,128)(2,1)S(1)} %get-tuple-element.11.back_right, s32[2,8,128]{2,1,0:T(8,128)S(1)} %get-tuple-element.12.masks), custom_call_target="tpu_custom_call" | custom-call | tf_op jit(solution)/shard_map/pallas_call | solution.py:417

commit v3 on v2

v3 whole, which is shorter than its diff:
```python
import jax
import jax.numpy as jnp
from jax import lax
from jax.experimental import pallas as pl
from jax.experimental.pallas import tpu as pltpu
from jax.sharding import PartitionSpec as P

MESH = pl.DeviceIdType.MESH
F32 = jnp.float32
BF16 = jnp.bfloat16
I32 = jnp.int32
NN = (((1,), (0,)), ((), ()))
NT = (((1,), (1,)), ((), ()))
G = 128


def dot(x, w, dims=NN):
    return lax.dot_general(x, w, dims, preferred_element_type=F32)


def split(x):
    high = x.astype(BF16)
    return high, (x - high.astype(F32)).astype(BF16)


def dot3(x, w, dims=NN):
    rows = x[0].shape[0]
    both = dot(jnp.concatenate(x, axis=0), w[0], dims)
    return both[:rows] + both[rows:] + dot(x[0], w[1], dims)


def beside(left, right):
    return jnp.concatenate([left, right], axis=1)


def above(top, bottom):
    return jnp.concatenate([top, bottom], axis=0)


def complex_split(real, imag):
    real_high, real_low = split(real)
    imag_high, imag_low = split(imag)
    return (real_high, imag_high), (real_low, imag_low)


def left_form(pieces):
    return tuple(beside(real, imag) for real, imag in pieces)


def right_form(pieces):
    return tuple(above(beside(real, imag), beside(-imag, real)) for real, imag in pieces)


def row_form(pieces):
    return tuple(above(beside(real, -imag), beside(imag, real)) for real, imag in pieces)


def complex_product(left, right):
    out = dot3(left_form(left), right_form(right))
    return complex_split(out[:, :G], out[:, G:])


def fields(index):
    return index >> 7, (index >> 5) & 3, (index >> 2) & 7, (index >> 1) & 1, index & 1


def exchange_lane(first, second, lane, low_bound, high_bound):
    rolled_first = pltpu.roll(first, G // 2, axis=1)
    rolled_second = pltpu.roll(second, G // 2, axis=1)
    return (
        jnp.where(lane < low_bound, first, rolled_second),
        jnp.where(lane >= high_bound, second, rolled_first),
    )


def travel_kernel(
    state_ref,
    gates_ref,
    low_ref,
    mid_ref,
    top_ref,
    swap_hbm,
    order_hbm,
    land,
    back_left,
    back_right,
    masks,
    gate,
    vector,
    other,
    send,
    angles,
    turns,
    other_turns,
    top_value,
    swap_ref,
    order_ref,
    load_sem,
    pair_sem,
    row_sem,
    relay_sem,
    gift_send,
    gift_recv,
    send_sem,
    recv_sem,
):
    wide = lax.axis_index("wide")
    mid = lax.axis_index("mid")
    low = lax.axis_index("low")
    depth = wide // 4
    across = lax.rem(wide, 4)
    core = lax.rem(mid, 2)
    place_x = low * 4 + across

    def peer(x, z):
        return (z * 4 + lax.rem(x, 4), mid, x // 4)

    def signal(semaphore, device):
        pl.semaphore_signal(semaphore, inc=1, device_id=device, device_id_type=MESH)

    partner = (wide, mid + 1 - 2 * core, low)

    leads = core == 1
    follows = core == 0
    has_corner = mid < 2
    is_corner = has_corner & (place_x == 0) & (depth == 0)

    barrier = pltpu.get_barrier_semaphore()

    @pl.when(leads)
    def greet_partner():
        signal(barrier, partner)

    def load(source, target, number):
        copy = pltpu.make_async_copy(source, target, load_sem.at[number])
        copy.start()
        return copy

    small = [
        load(swap_hbm, swap_ref, 3),
        load(order_hbm, order_ref, 4),
        load(low_ref, angles.at[pl.ds(0, 1)], 5),
        load(mid_ref, angles.at[pl.ds(1, 1)], 6),
        load(top_ref, top_value, 7),
    ]
    first_gates = load(gates_ref.at[pl.ds(0, 4)], gate.at[pl.ds(0, 4)], 0)
    load_state = load(state_ref, vector, 1)
    last_gates = load(gates_ref.at[pl.ds(4, 6)], gate.at[pl.ds(4, 6)], 2)

    @pl.when(follows)
    def answer_partner():
        pl.semaphore_wait(barrier, 1)
        signal(pair_sem.at[0], partner)

    @pl.when(leads & jnp.logical_not(is_corner))
    def meet_partner():
        pl.semaphore_wait(pair_sem.at[0], 1)

    @pl.when(leads)
    def greet_peers():
        for step in range(1, 8):
            signal(barrier, peer(lax.rem(place_x + step, 8), depth))

        @pl.loop(depth + 1, 8)
        def greet_higher(z):
            for x in range(8):
                signal(barrier, peer(x, z))

    @pl.when(leads & is_corner)
    def meet_late_partner():
        pl.semaphore_wait(pair_sem.at[0], 1)

    def gift(source, target, number):
        copy = pltpu.make_async_remote_copy(
            src_ref=source,
            dst_ref=target,
            send_sem=gift_send.at[number],
            recv_sem=gift_recv.at[number],
            device_id=partner,
            device_id_type=MESH,
        )
        copy.start()
        return copy

    state_gift = gift(state_ref, other, 0)

    for copy in small:
        copy.wait()
    angle = angles[...]
    line = lax.broadcasted_iota(I32, (8, G), 0)
    angle = jnp.where(
        line == 0,
        angle[0:1] + jnp.zeros((8, G), F32),
        jnp.where(line == 1, angle[1:2], top_value[0, 0, 0, 0]),
    )
    turns[0] = jnp.cos(angle)
    turns[1] = jnp.sin(angle)
    turn_gift = gift(turns, other_turns, 1)

    first_swap = swap_ref[0]
    second_swap = swap_ref[1]
    low_bound = jnp.where(second_swap == 0, G // 2, G)
    high_bound = jnp.where(second_swap == 0, G // 2, 0)
    lane = lax.broadcasted_iota(I32, (G, G), 1)
    short_lane = lax.broadcasted_iota(I32, (8, G), 1)
    masks[0] = jnp.where(short_lane < low_bound, 1, 0)
    masks[1] = jnp.where(short_lane >= high_bound, 1, 0)

    swapped = first_swap + 1
    weights = []
    holds = []
    for place in range(4):
        source = order_ref[place]
        is_swapped = source == swapped
        weights.append(jnp.where(is_swapped, 0, jnp.left_shift(8, source)))
        holds.append(jnp.where(is_swapped, 1, 0))
    low_weight = jnp.where(second_swap == 2, 2, 1)
    spare_weight = 3 - low_weight
    core_part = core * jnp.left_shift(8, swapped)
    row = lax.broadcasted_iota(I32, (2 * G, G), 0)
    column = lax.broadcasted_iota(I32, (2 * G, G), 1)
    low_bit, x_hi, z_bits, part, spare = fields(row)
    source = low_bit * low_weight + spare * spare_weight + (x_hi & 1) * 4 + core_part
    held = jnp.zeros_like(source)
    bits = (x_hi >> 1, z_bits & 1, (z_bits >> 1) & 1, z_bits >> 2)
    for bit, weight, hold in zip(bits, weights, holds):
        source = source + bit * weight
        held = held + bit * hold
    picks = jnp.where(source == column, 1.0, 0.0).astype(BF16)
    is_own = held == core
    is_real = part == 0

    low_cos, low_sin = turns[0, 0:1, :], turns[1, 0:1, :]
    mid_cos, mid_sin = turns[0, 1:2, :], turns[1, 1:2, :]

    def turned(real, imag, cosine, sine):
        return complex_split(real * cosine - imag * sine, real * sine + imag * cosine)

    first_gates.wait()
    inner = complex_product(
        turned(gate[2, 0], gate[2, 1], low_cos, low_sin), complex_split(gate[0, 0], gate[0, 1])
    )
    three_high, three_low = complex_split(gate[3, 0], gate[3, 1])
    picked = (
        dot(picks, beside(*three_high)).astype(BF16),
        dot(picks, beside(*three_low)).astype(BF16),
    )
    outer = dot3(picked, right_form(turned(gate[1, 0], gate[1, 1], mid_cos, mid_sin)))
    outer = split(
        beside(
            jnp.where(is_real, outer[:, :G], outer[:, G:]),
            jnp.where(is_real, -outer[:, G:], outer[:, :G]),
        )
    )
    load_state.wait()
    own = left_form(turned(vector[0], vector[1], turns[0, 2:3, :], turns[1, 2:3, :]))

    @pl.when(leads)
    def meet_peers():
        pl.semaphore_wait(barrier, 8 * depth + 7)
        signal(pair_sem.at[0], partner)

        @pl.loop(0, depth)
        def answer_lower(z):
            for x in range(8):
                signal(row_sem.at[depth], peer(x, z))

        @pl.when(is_corner)
        def tell_row():
            for x in range(1, 8):
                signal(row_sem.at[8], peer(x, depth))

    turn_gift.wait_recv()
    state_gift.wait_recv()
    far = left_form(turned(other[0], other[1], other_turns[0, 2:3, :], other_turns[1, 2:3, :]))
    value = dot3(
        tuple(above(mine, theirs) for mine, theirs in zip(own, far)), row_form(inner), NT
    )
    value = above(beside(value[:G, :G], value[G:, :G]), beside(value[:G, G:], value[G:, G:]))
    front = dot3(outer, split(value))
    rows = jnp.where(is_own, front[:, :G], front[:, G:])
    first, second = exchange_lane(rows[:G], rows[G:], lane, low_bound, high_bound)
    send[:G] = first
    send[G:] = second
    mine = place_x * 8 + depth

    def block(slot):
        return pl.ds(pl.multiple_of(slot * 4, 4), 4)

    def travel(x, z):
        slot = x * 8 + z
        return pltpu.make_async_remote_copy(
            src_ref=send.at[block(slot), :],
            dst_ref=land.at[block(mine), :],
            send_sem=send_sem.at[slot],
            recv_sem=recv_sem.at[mine],
            device_id=peer(x, z),
            device_id_type=MESH,
        )

    @pl.when(follows)
    def await_row():
        pl.semaphore_wait(pair_sem.at[0], 1)

    @pl.loop(0, depth + 1)
    def send_lower(z):
        for step in (4, 3, 5, 2, 6, 1, 7, 0):
            x = lax.rem(place_x + step, 8)
            late = has_corner & follows & (x == 0) & (z == 0)

            @pl.when(jnp.logical_not(late | ((z == depth) & (x == place_x))))
            def send_one():
                travel(x, z).start()

    stay = pltpu.make_async_copy(send.at[block(mine), :], land.at[block(mine), :], load_sem.at[0])
    stay.start()

    @pl.loop(depth + 1, 8)
    def send_higher(z):
        @pl.when(leads)
        def relay_higher():
            pl.semaphore_wait(row_sem.at[z], 8)
            signal(relay_sem.at[z], partner)

        @pl.when(follows)
        def await_higher():
            pl.semaphore_wait(relay_sem.at[z], 1)

        for step in (4, 3, 5, 2, 6, 1, 7, 0):
            travel(lax.rem(place_x + step, 8), z).start()

        @pl.when(leads & is_corner)
        def tell_higher():
            for x in range(8):
                signal(row_sem.at[8], peer(x, z))

    last_gates.wait()

    def pieces(number):
        return complex_split(gate[number, 0], gate[number, 1])

    inner = complex_product(pieces(8), complex_product(pieces(6), pieces(4)))
    for level, value in enumerate(row_form(inner)):
        back_right[level] = value

    target = lax.broadcasted_iota(I32, (2 * G, 2 * G), 0)
    low_bit, x_hi, z_bits, part, spare = fields(
        lax.broadcasted_iota(I32, (2 * G, 2 * G), 1)
    )
    source = low_bit * low_weight + spare * spare_weight + x_hi * 4 + z_bits * 16 + part * G
    order = jnp.where(source == target, 1.0, 0.0).astype(BF16)
    outer = complex_product(pieces(9), complex_product(pieces(7), pieces(5)))
    for level, value in enumerate(row_form(outer)):
        back_left[level] = dot(value, order).astype(BF16)

    @pl.when(has_corner & jnp.logical_not(is_corner) & leads)
    def relay_corner():
        pl.semaphore_wait(row_sem.at[8], 1)
        signal(relay_sem.at[8], partner)

    @pl.when(has_corner & jnp.logical_not(is_corner) & follows)
    def send_corner():
        pl.semaphore_wait(relay_sem.at[8], 1)
        travel(0, 0).start()

    stay.wait()

    @pl.loop(1, 64)
    def await_others(step):
        slot = lax.rem(mine + step, 64)
        copy = pltpu.make_async_remote_copy(
            src_ref=send.at[block(slot), :],
            dst_ref=land.at[block(slot), :],
            send_sem=send_sem.at[slot],
            recv_sem=recv_sem.at[slot],
            device_id=peer(slot // 8, lax.rem(slot, 8)),
            device_id_type=MESH,
        )
        copy.wait_send()
        copy.wait_recv()

    state_gift.wait_send()
    turn_gift.wait_send()


def final_kernel(landed, back_left, back_right, masks, out_ref):
    keep_first = jnp.concatenate([masks[0]] * 16, axis=0) > 0
    keep_second = jnp.concatenate([masks[1]] * 16, axis=0) > 0
    first, second = landed[:G], landed[G:]
    rolled_first = pltpu.roll(first, G // 2, axis=1)
    rolled_second = pltpu.roll(second, G // 2, axis=1)
    stacked = above(
        jnp.where(keep_first, first, rolled_second),
        jnp.where(keep_second, second, rolled_first),
    )
    middle = dot3((back_left[0], back_left[1]), split(stacked))
    result = dot3(
        left_form(complex_split(middle[:G], middle[G:])), (back_right[0], back_right[1]), NT
    )
    out_ref[0] = result[:, :G]
    out_ref[1] = result[:, G:]


def on_device(state, gates, phase_low, phase_mid, phase_top, swap_qubits, regroup_order):
    square = (2, G, G)
    doubled = (2, 2 * G, 2 * G)
    vmem = pl.BlockSpec(memory_space=pltpu.VMEM)
    hbm = pl.BlockSpec(memory_space=pltpu.HBM)
    between = pl.pallas_call(
        travel_kernel,
        out_shape=(
            pltpu.VMEM((2 * G, G), F32),
            pltpu.VMEM(doubled, BF16),
            pltpu.VMEM(doubled, BF16),
            pltpu.VMEM((2, 8, G), I32),
        ),
        in_specs=[hbm] * 7,
        out_specs=(vmem,) * 4,
        scratch_shapes=[
            pltpu.VMEM(gates.shape, F32),
            pltpu.VMEM(square, F32),
            pltpu.VMEM(square, F32),
            pltpu.VMEM((2 * G, G), F32),
            pltpu.VMEM((2, G), F32),
            pltpu.VMEM((2, 8, G), F32),
            pltpu.VMEM((2, 8, G), F32),
            pltpu.SMEM((1, 1, 1, 1), F32),
            pltpu.SMEM((2,), I32),
            pltpu.SMEM((4,), I32),
            pltpu.SemaphoreType.DMA((8,)),
            pltpu.SemaphoreType.REGULAR((1,)),
            pltpu.SemaphoreType.REGULAR((9,)),
            pltpu.SemaphoreType.REGULAR((9,)),
            pltpu.SemaphoreType.DMA((2,)),
            pltpu.SemaphoreType.DMA((2,)),
            pltpu.SemaphoreType.DMA((64,)),
            pltpu.SemaphoreType.DMA((64,)),
        ],
        compiler_params=pltpu.CompilerParams(collective_id=0, has_side_effects=True),
    )(
        state.reshape(square),
        gates,
        phase_low.reshape(1, G),
        phase_mid.reshape(1, G),
        phase_top,
        swap_qubits,
        regroup_order,
    )
    out = pl.pallas_call(
        final_kernel,
        out_shape=jax.ShapeDtypeStruct(square, F32),
        in_specs=[vmem] * 4,
        out_specs=vmem,
        compiler_params=pltpu.CompilerParams(vmem_limit_bytes=8 << 20),
    )(*between)
    return out.reshape(state.shape)


def solution(mesh):
    return jax.shard_map(
        on_device,
        mesh=mesh,
        in_specs=(
            P(None, "wide", "mid", "low", None),
            P(),
            P(),
            P(),
            P("wide", "mid", "low", None),
            P(),
            P(),
        ),
        out_specs=P(None, "wide", "mid", "low", None),
        check_vma=False,
    )
```

time: 33.4 us -> 29.6 us (0.89)
  Pallas kernels: 32.6 us -> 28.7 us
    pallas_call x1, Pallas kernels: 31.4 us -> 27.5 us  [on_device(): pl.pallas_call(travel_kernel, out_shape=(pltpu.VMEM((2 * G, G), F32), plt...]
where the time goes in v3:
time: 29.6 us; the launch traced here: 29.4 us
  Pallas kernels  28.7 us (97%)
  between operations  0.66 us (2%)
    pallas_call x1, Pallas kernels, on_device(): pl.pallas_call(travel_kernel, out_shape=(pltpu.VMEM((2 * G, G), F32), plt...  27.5 us
    pallas_call x1, Pallas kernels, on_device(): pl.pallas_call(final_kernel, out_shape=jax.ShapeDtypeStruct(square, F32),...  1.21 us

profile of v3, /device:TPU:1, one launch (start us, length us, event | category | flops | bytes accessed | tf_op | source)
XLA Modules:
  0.0 29.4 jit_solution(8838063089501767845)
XLA Ops:
  0.7 27.5 %shard_map.73 = (f32[256,128]{1,0:T(8,128)S(1)}, bf16[2,256,256]{2,1,0:T(8,128)(2,1)S(1)}, bf16[2,256,256]{2,1,0:T(8,128)(2,1)S(1)}, s32[2,8,128]{2,1,0:T(8,128)S(1)}) custom-call(f32[2,128,128]{2,1,0:T(8,128)} %bitcast.4, f32[10,2,128,128]{3,2,1,0:T(8,128)} %gates_ref.1, f32[1,128]{1,0:T(1,128)} %bitcast.5, f32[1,128]{1,0:T(1,128)} %bitcast.6, ...), custom_call_target="tpu_custom_call" | custom-call | tf_op jit(solution)/shard_map/pallas_call | solution.py:409
  28.2 1.2 %shard_map.74 = f32[2,128,128]{2,1,0:T(8,128)} custom-call(f32[256,128]{1,0:T(8,128)S(1)} %get-tuple-element.9.landed, bf16[2,256,256]{2,1,0:T(8,128)(2,1)S(1)} %get-tuple-element.10.back_left, bf16[2,256,256]{2,1,0:T(8,128)(2,1)S(1)} %get-tuple-element.11.back_right, s32[2,8,128]{2,1,0:T(8,128)S(1)} %get-tuple-element.12.masks), custom_call_target="tpu_custom_call" | custom-call | tf_op jit(solution)/shard_map/pallas_call | solution.py:449

commit v4 on v3

--- a/solution.py
+++ b/solution.py
@@ -292,8 +292,8 @@
         return pltpu.make_async_remote_copy(
             src_ref=send.at[block(slot), :],
             dst_ref=land.at[block(mine), :],
-            send_sem=send_sem.at[slot],
-            recv_sem=recv_sem.at[mine],
+            send_sem=send_sem,
+            recv_sem=recv_sem,
             device_id=peer(x, z),
             device_id_type=MESH,
         )
@@ -312,8 +312,7 @@
             def send_one():
                 travel(x, z).start()
 
-    stay = pltpu.make_async_copy(send.at[block(mine), :], land.at[block(mine), :], load_sem.at[0])
-    stay.start()
+    pltpu.make_async_copy(send.at[block(mine), :], land.at[block(mine), :], recv_sem).start()
 
     @pl.loop(depth + 1, 8)
     def send_higher(z):
@@ -363,22 +362,9 @@
         pl.semaphore_wait(relay_sem.at[8], 1)
         travel(0, 0).start()
 
-    stay.wait()
-
-    @pl.loop(1, 64)
-    def await_others(step):
-        slot = lax.rem(mine + step, 64)
-        copy = pltpu.make_async_remote_copy(
-            src_ref=send.at[block(slot), :],
-            dst_ref=land.at[block(slot), :],
-            send_sem=send_sem.at[slot],
-            recv_sem=recv_sem.at[slot],
-            device_id=peer(slot // 8, lax.rem(slot, 8)),
-            device_id_type=MESH,
-        )
-        copy.wait_send()
-        copy.wait_recv()
-
+    pltpu.make_async_copy(send, land, recv_sem).wait()
+    others = pl.ds(0, 2 * G - 4)
+    pltpu.make_async_copy(send.at[others, :], land.at[others, :], send_sem).wait()
     state_gift.wait_send()
     turn_gift.wait_send()
 
@@ -433,8 +419,8 @@
             pltpu.SemaphoreType.REGULAR((9,)),
             pltpu.SemaphoreType.DMA((2,)),
             pltpu.SemaphoreType.DMA((2,)),
-            pltpu.SemaphoreType.DMA((64,)),
-            pltpu.SemaphoreType.DMA((64,)),
+            pltpu.SemaphoreType.DMA,
+            pltpu.SemaphoreType.DMA,
         ],
         compiler_params=pltpu.CompilerParams(collective_id=0, has_side_effects=True),
     )(

time: 29.6 us -> 27.9 us (0.943)
  Pallas kernels: 28.7 us -> 27.1 us
    pallas_call x1, Pallas kernels: 27.5 us -> 25.8 us  [on_device(): pl.pallas_call(travel_kernel, out_shape=(pltpu.VMEM((2 * G, G), F32), plt...]
where the time goes in v4:
time: 27.9 us; the launch traced here: 27.7 us
  Pallas kernels  27.1 us (97%)
  between operations  0.66 us (2%)
    pallas_call x1, Pallas kernels, on_device(): pl.pallas_call(travel_kernel, out_shape=(pltpu.VMEM((2 * G, G), F32), plt...  25.8 us
    pallas_call x1, Pallas kernels, on_device(): pl.pallas_call(final_kernel, out_shape=jax.ShapeDtypeStruct(square, F32),...  1.22 us

profile of v4, /device:TPU:1, one launch (start us, length us, event | category | flops | bytes accessed | tf_op | source)
XLA Modules:
  0.0 27.7 jit_solution(11341900784626188020)
XLA Ops:
  0.7 25.8 %shard_map.73 = (f32[256,128]{1,0:T(8,128)S(1)}, bf16[2,256,256]{2,1,0:T(8,128)(2,1)S(1)}, bf16[2,256,256]{2,1,0:T(8,128)(2,1)S(1)}, s32[2,8,128]{2,1,0:T(8,128)S(1)}) custom-call(f32[2,128,128]{2,1,0:T(8,128)} %bitcast.4, f32[10,2,128,128]{3,2,1,0:T(8,128)} %gates_ref.1, f32[1,128]{1,0:T(1,128)} %bitcast.5, f32[1,128]{1,0:T(1,128)} %bitcast.6, ...), custom_call_target="tpu_custom_call" | custom-call | tf_op jit(solution)/shard_map/pallas_call | solution.py:395
  26.5 1.2 %shard_map.74 = f32[2,128,128]{2,1,0:T(8,128)} custom-call(f32[256,128]{1,0:T(8,128)S(1)} %get-tuple-element.9.landed, bf16[2,256,256]{2,1,0:T(8,128)(2,1)S(1)} %get-tuple-element.10.back_left, bf16[2,256,256]{2,1,0:T(8,128)(2,1)S(1)} %get-tuple-element.11.back_right, s32[2,8,128]{2,1,0:T(8,128)S(1)} %get-tuple-element.12.masks), custom_call_target="tpu_custom_call" | custom-call | tf_op jit(solution)/shard_map/pallas_call | solution.py:435
